TPU v7x, 512 devices: a whole 4x8x8 slice. The times are simulated.
512 devices in a mesh: dp: 16 (over x, z_hi), tm: 32 (over z_lo, y, core).
Axes of the slice: x: 4, y: 8, z: 8 (z_hi: 4, z_lo: 2; z = z_hi * 2 + z_lo), core: 2. Of those that a mesh axis runs over, the one named last changes fastest.
Arguments:
- activations: bfloat16 [16, 64, 64, 16, 128], P('dp', 'tm')
- conv_weight: bfloat16 [3, 3, 3, 128, 128], replicated, may hold values from -0.109375 to 0.109375
- norm_gain: float32 [128], replicated, may hold values from 0.5 to 1.5
- norm_bias: float32 [128], replicated, may hold values from -0.5 to 0.5
- down_weight: bfloat16 [3, 3, 128, 128], replicated, may hold values from -0.1875 to 0.1875
- cotangent: bfloat16 [16, 64, 32, 8, 128], P('dp', None, 'tm'), may hold values from -0.21875 to 0.21875
Outputs:
- encoded: bfloat16 [16, 64, 32, 8, 128], P('dp', None, 'tm')
- grad_down: float32 [3, 3, 128, 128], P(None, None, None, 'tm')
All inputs are finite; a program needn't handle non-finite values.
Results may differ from a plain program's by a relative error of at most 0.005.
Values may be sent and summed in bfloat16 or wider, within the bound.
A program may use at most 64 MiB of HBM per device.

v0:
```python
import jax
import jax.numpy as jnp
from jax import lax
from jax.sharding import PartitionSpec as P

G = 32


def passed_along(shard, axis, by):
    count = lax.axis_size(axis)
    pairs = [(i, i + by) for i in range(count) if 0 <= i + by < count]
    return lax.ppermute(shard, axis, pairs)


def down_patches(extended, rows_out, cols_out):
    tap_list = []
    for row_tap in range(3):
        for col_tap in range(3):
            tap_list.append(
                extended[
                    :,
                    :,
                    row_tap : row_tap + 2 * rows_out - 1 : 2,
                    col_tap : col_tap + 2 * cols_out - 1 : 2,
                    :,
                ]
            )
    return jnp.concatenate(tap_list, axis=-1)


def per_device(activations, conv_weight, norm_gain, norm_bias, down_weight, cotangent):
    clip_count, frames_dev, height, width_cells, channels = activations.shape
    out_channels = conv_weight.shape[-1]
    groups = G
    earlier = passed_along(activations, "tm", 1)
    framed = jnp.concatenate([earlier, activations], axis=1)
    framed = jnp.pad(framed, ((0, 0), (0, 0), (1, 1), (1, 1), (0, 0)))
    conv_out = jnp.zeros(
        (clip_count * frames_dev * height * width_cells, out_channels), jnp.float32
    )
    for row_tap in range(3):
        for col_tap in range(3):
            window_slab = framed[
                :, :, row_tap : row_tap + height, col_tap : col_tap + width_cells, :
            ]
            stacked = jnp.concatenate(
                [window_slab[:, time_tap : time_tap + frames_dev] for time_tap in range(3)], axis=-1
            )
            tap_weight = conv_weight[:, row_tap, col_tap].reshape(3 * channels, out_channels)
            conv_out = conv_out + jnp.dot(
                stacked.reshape(-1, 3 * channels), tap_weight, preferred_element_type=jnp.float32
            )
    grouped = conv_out.reshape(
        clip_count, frames_dev, height, width_cells, groups, channels // groups
    )
    group_sums = jnp.sum(grouped, axis=(1, 2, 3, 5))
    group_squares = jnp.sum(grouped * grouped, axis=(1, 2, 3, 5))
    group_sums, group_squares = lax.psum((group_sums, group_squares), "tm")
    members = float(frames_dev * lax.axis_size("tm") * height * width_cells * (channels // groups))
    group_mean = group_sums / members
    variance = group_squares / members - group_mean * group_mean
    inverse = lax.rsqrt(variance + 1e-06)
    normed = (
        (grouped - group_mean[:, None, None, None, :, None]) * inverse[:, None, None, None, :, None]
    ).reshape(clip_count, frames_dev, height, width_cells, channels) * norm_gain + norm_bias
    hidden = jax.nn.silu(normed).astype(jnp.bfloat16)
    down_flat = down_weight.reshape(9 * channels, -1)
    row_local = lax.all_to_all(hidden, "tm", split_axis=2, concat_axis=1, tiled=True)
    lower_row = passed_along(row_local[:, :, :1], "tm", -1)
    extended = jnp.concatenate([row_local, lower_row], axis=2)
    extended = jnp.pad(extended, ((0, 0), (0, 0), (0, 0), (0, 1), (0, 0)))
    patches = down_patches(extended, row_local.shape[2] // 2, width_cells // 2)
    encoded = (
        jnp.dot(patches.reshape(-1, 9 * channels), down_flat, preferred_element_type=jnp.float32)
        .reshape(cotangent.shape)
        .astype(jnp.bfloat16)
    )
    partial_value = lax.dot_general(
        patches.reshape(-1, 9 * channels),
        cotangent.reshape(-1, cotangent.shape[-1]),
        (((0,), (0,)), ((), ())),
        preferred_element_type=jnp.float32,
    )
    partial_value = partial_value.reshape(3, 3, channels, -1)
    shares = lax.psum_scatter(partial_value, "tm", scatter_dimension=3, tiled=True)
    grad_down = lax.psum(shares, "dp")
    return (encoded, grad_down)


def solution(mesh):
    placed = (P("dp", "tm", None, None, None), P(), P(), P(), P(), P("dp", None, "tm", None, None))
    return jax.shard_map(
        per_device,
        mesh=mesh,
        in_specs=placed,
        out_specs=(P("dp", None, "tm", None, None), P(None, None, None, "tm")),
        check_vma=False,
    )
```

profile of v0, /device:TPU:64, one launch (start us, length us, event | category | flops | bytes accessed | tf_op | source)
XLA Modules:
  0.0 432.4 jit_solution(16287270471883125071)
XLA Ops:
  7.2 2.1 collective-permute-start
  9.3 1.3 fusion.17
  10.6 9.6 %collective-permute-done = bf16[1,2,64,16,128]{4,3,2,1,0:T(8,128)(2,1)S(1)} collective-permute-done((bf16[1,2,64,16,128]{4,3,2,1,0:T(8,128)(2,1)}, bf16[1,2,64,16,128]{4,3,2,1,0:T(8,128)(2,1)S(1)}, u32[]{:S(2)}, u32[]{:S(2)}) %collective-permute-start) | collective-permute-done | bytes 524320 | tf_op jit(solution)/shard_map/ppermute | solution.py:12
  20.3 3.1 pad_slice_fusion.2
  23.4 0.6 pad_slice_fusion.1
  25.1 0.6 convolution_add_fusion.7
  26.1 0.6 convolution_add_fusion.6
  28.5 0.6 convolution_add_fusion.3
  30.1 0.6 convolution_add_fusion.1
  30.7 0.7 fusion.16
  31.9 53.0 %all-reduce.3 = (f32[1,32]{1,0:T(1,128)S(1)}, f32[1,32]{1,0:T(1,128)S(1)}) all-reduce(f32[1,32]{1,0:T(1,128)S(1)} %bitcast.101, f32[1,32]{1,0:T(1,128)S(1)} %bitcast.100), channel_id=1, replica_groups=mesh['dp'=16,'tm'=32] {'tm'}, use_global_device_ids=true, to_apply=%region_5.6 | all-reduce | flops 64 | bytes 512 | tf_op jit(solution)/shard_map/psum | solution.py:58
  85.6 20.5 %all_to_all.18 = bf16[1,2,64,16,128]{4,3,1,0,2:T(8,128)(2,1)S(1)} all-to-all(bf16[1,2,64,16,128]{4,3,1,0,2:T(8,128)(2,1)S(1)} %multiply_convert_fusion), channel_id=1, replica_groups=mesh['dp'=16,'tm'=32] {'tm'}, dimensions={2} | all-to-all | bytes 1048576 | tf_op jit(solution)/shard_map/all_to_all | solution.py:68
  106.1 2.1 collective-permute-start.1
  108.2 3.7 collective-permute-done.1
  112.9 0.7 slice.213
  114.5 0.7 slice.216
  116.0 0.7 slice.219
  117.1 0.6 copy.18
  117.9 1.3 fusion.14
  119.2 1.3 dynamic-slice
  121.1 1.1 fusion.8
  122.3 220.0 %all-reduce.6.cloned.1.call-done = f32[3,3,128,128]{2,3,1,0:T(8,128)} async-done(((f32[3,3,128,128]{2,3,1,0:T(8,128)}), f32[3,3,128,128]{2,3,1,0:T(8,128)}) %all-reduce.6.cloned.1.call-update) | async-done | bytes 589840
  342.3 0.8 constant_dynamic-slice_fusion
  343.0 82.5 %psum.23 = f32[3,3,128,4]{2,3,1,0:T(4,128)} all-reduce(f32[3,3,128,4]{2,3,1,0:T(4,128)S(1)} %constant_dynamic-slice_fusion), channel_id=1, replica_groups=mesh['dp'=16,'tm'=32] {'dp'}, use_global_device_ids=true, to_apply=%region_7.8 | all-reduce | flops 4608 | bytes 36864 | tf_op jit(solution)/shard_map/psum | solution.py:86
  (51 shorter events, 8.7 us)
Async XLA Ops:
  7.2 114.0 %copy-start = (bf16[3,3,128,128]{3,2,1,0:T(8,128)(2,1)S(1)}, bf16[3,3,128,128]{3,2,1,0:T(8,128)(2,1)}, u32[]{:S(2)}) copy-start(bf16[3,3,128,128]{3,2,1,0:T(8,128)(2,1)} %param.10) | copy-start | bytes 884740
  7.2 13.0 %copy-start.1 = (bf16[1,2,64,16,128]{4,3,2,1,0:T(8,128)(2,1)S(1)}, bf16[1,2,64,16,128]{4,3,2,1,0:T(8,128)(2,1)}, u32[]{:S(2)}) copy-start(bf16[1,2,64,16,128]{4,3,2,1,0:T(8,128)(2,1)} %param.6) | copy-start | bytes 1572868
  7.2 335.1 %all-reduce.6.cloned.1.call-start = ((), (), s32[]{:S(2)}) async-start(), calls=%async_computation.1 | async-start | bytes 1179648
  7.2 13.0 %collective-permute-start = (bf16[1,2,64,16,128]{4,3,2,1,0:T(8,128)(2,1)}, bf16[1,2,64,16,128]{4,3,2,1,0:T(8,128)(2,1)S(1)}, u32[]{:S(2)}, u32[]{:S(2)}) collective-permute-start(bf16[1,2,64,16,128]{4,3,2,1,0:T(8,128)(2,1)} %param.6), channel_id=1, source_target_pairs={{0,1},{1,2},{2,3},{3,4},{4,5},{5,6},{6,7},{7,8},{8,9},{9,10},{10,1... | collective-permute-start | bytes 1572872 | tf_op jit(solution)/shard_map/ppermute | solution.py:12
  30.7 54.5 %copy-start.3 = (f32[128]{0:T(128)S(1)}, f32[128]{0:T(128)}, u32[]{:S(2)}) copy-start(f32[128]{0:T(128)} %param.9) | copy-start | bytes 1540
  30.7 54.5 %copy-start.4 = (f32[128]{0:T(128)S(1)}, f32[128]{0:T(128)}, u32[]{:S(2)}) copy-start(f32[128]{0:T(128)} %param.8) | copy-start | bytes 1540
  106.1 5.8 %collective-permute-start.1 = (bf16[1,64,1,16,128]{4,3,1,2,0:T(8,128)(2,1)S(1)}, bf16[1,64,1,16,128]{4,3,1,2,0:T(8,128)(2,1)S(1)}, u32[]{:S(2)}, u32[]{:S(2)}) collective-permute-start(bf16[1,64,1,16,128]{4,3,1,2,0:T(8,128)(2,1)S(1)} %slice.221), channel_id=1, source_target_pairs={{1,0},{2,1},{3,2},{4,3},{5,4},{6,5},{7,6},{8,7},{9,8},{10,9},{11,1... | collective-permute-start | bytes 786440 | tf_op jit(solution)/shard_map/ppermute | solution.py:12
  117.0 0.9 copy-start.2
Sparse Core Ops, SparseCore 0:
  119.3 222.8 all-reduce.5
where the time goes:
time: 433 us; the launch traced here: 432 us
  waiting for transfers between devices  233 us (54%)
  blocking collectives  156 us (36%)
  between operations  15.1 us (3%)
  local copies, waits for them, and re-layouts  13.4 us (3%)
  matrix products  7.8 us (2%)
    unnamed x2, waiting for transfers between devices  220 us
    psum x1, blocking collectives, per_device(): grad_down = lax.psum(shares, 'dp')  82.5 us
    psum x1, blocking collectives, per_device(): group_sums, group_squares = lax.psum((group_sums, group_squares), 'tm')  53 us
    all_to_all x1, blocking collectives, per_device(): lax.all_to_all(hidden, 'tm', split_axis=2, concat_axis=1, tiled=True)  20.5 us
    ppermute x2, waiting for transfers between devices, passed_along(): return lax.ppermute(shard, axis, pairs)  13.3 us
  transfers between devices with their start and end apart: 3, of which 3 were waited for; matrix products, arithmetic and copies ran while one was open for 1% of the time, Pallas kernels for 0%

commit v1 on v0

--- a/solution.py
+++ b/solution.py
@@ -83,7 +83,7 @@
     )
     partial_value = partial_value.reshape(3, 3, channels, -1)
     shares = lax.psum_scatter(partial_value, "tm", scatter_dimension=3, tiled=True)
-    grad_down = lax.psum(shares, "dp")
+    grad_down = jnp.sum(lax.all_gather(shares, "dp"), axis=0)
     return (encoded, grad_down)
 
 

time: 433 us -> 396 us (0.915)
  blocking collectives: 156 us -> 119 us
    psum x1 -> x0, blocking collectives: 82.5 us -> none  [per_device(): grad_down = lax.psum(shares, 'dp')]
    all_gather x0 -> x1, blocking collectives: none -> 45.4 us  [per_device(): grad_down = jnp.sum(lax.all_gather(shares, 'dp'), axis=0)]
where the time goes in v1:
time: 396 us
  waiting for transfers between devices  233 us (59%)
  blocking collectives  119 us (30%)
  between operations  15.1 us (4%)
  local copies, waits for them, and re-layouts  13.4 us (3%)
  matrix products  7.8 us (2%)
  starting transfers between devices  4.19 us (1%)
    unnamed x2, waiting for transfers between devices  220 us
    psum x1, blocking collectives, per_device(): group_sums, group_squares = lax.psum((group_sums, group_squares), 'tm')  53 us
    all_gather x1, blocking collectives, per_device(): grad_down = jnp.sum(lax.all_gather(shares, 'dp'), axis=0)  45.4 us
    all_to_all x1, blocking collectives, per_device(): lax.all_to_all(hidden, 'tm', split_axis=2, concat_axis=1, tiled=True)  20.5 us
    ppermute x2, waiting for transfers between devices, passed_along(): return lax.ppermute(shard, axis, pairs)  13.3 us
  transfers between devices with their start and end apart: 3, of which 3 were waited for; matrix products, arithmetic and copies ran while one was open for 1% of the time, Pallas kernels for 0%

profile of v1, /device:TPU:64, one launch (start us, length us, event | category | flops | bytes accessed | tf_op | source)
XLA Modules:
  0.0 396.0 jit_solution(2410299195833913455)
XLA Ops:
  7.2 2.1 collective-permute-start
  9.3 1.3 fusion.17
  10.6 9.6 %collective-permute-done = bf16[1,2,64,16,128]{4,3,2,1,0:T(8,128)(2,1)S(1)} collective-permute-done((bf16[1,2,64,16,128]{4,3,2,1,0:T(8,128)(2,1)}, bf16[1,2,64,16,128]{4,3,2,1,0:T(8,128)(2,1)S(1)}, u32[]{:S(2)}, u32[]{:S(2)}) %collective-permute-start) | collective-permute-done | bytes 524320 | tf_op jit(solution)/shard_map/ppermute | solution.py:12
  20.3 3.1 pad_slice_fusion.2
  23.4 0.6 pad_slice_fusion.1
  26.1 0.6 convolution_add_fusion.6
  28.5 0.6 convolution_add_fusion.3
  30.1 0.6 convolution_add_fusion.1
  30.7 0.7 fusion.16
  31.9 53.0 %all-reduce.3 = (f32[1,32]{1,0:T(1,128)S(1)}, f32[1,32]{1,0:T(1,128)S(1)}) all-reduce(f32[1,32]{1,0:T(1,128)S(1)} %bitcast.103, f32[1,32]{1,0:T(1,128)S(1)} %bitcast.102), channel_id=1, replica_groups=mesh['dp'=16,'tm'=32] {'tm'}, use_global_device_ids=true, to_apply=%region_5.6 | all-reduce | flops 64 | bytes 512 | tf_op jit(solution)/shard_map/psum | solution.py:58
  85.6 20.5 %all_to_all.18 = bf16[1,2,64,16,128]{4,3,1,0,2:T(8,128)(2,1)S(1)} all-to-all(bf16[1,2,64,16,128]{4,3,1,0,2:T(8,128)(2,1)S(1)} %multiply_convert_fusion), channel_id=1, replica_groups=mesh['dp'=16,'tm'=32] {'tm'}, dimensions={2} | all-to-all | bytes 1048576 | tf_op jit(solution)/shard_map/all_to_all | solution.py:68
  106.1 2.1 collective-permute-start.1
  108.2 3.7 collective-permute-done.1
  112.9 0.7 slice.213
  114.5 0.7 slice.216
  116.0 0.7 slice.219
  117.1 0.6 copy.18
  117.9 1.3 fusion.14
  119.2 1.3 dynamic-slice
  121.1 1.1 fusion.8
  122.3 220.0 %all-reduce.6.cloned.1.call-done = f32[3,3,128,128]{2,3,1,0:T(8,128)} async-done(((f32[3,3,128,128]{2,3,1,0:T(8,128)}), f32[3,3,128,128]{2,3,1,0:T(8,128)}) %all-reduce.6.cloned.1.call-update) | async-done | bytes 589840
  342.3 0.8 constant_dynamic-slice_fusion
  343.0 45.4 %all-gather = f32[48,3,128,4]{2,3,1,0:T(4,128)S(1)} all-gather(f32[3,3,128,4]{2,3,1,0:T(4,128)S(1)} %constant_dynamic-slice_fusion), channel_id=2, replica_groups=mesh['dp'=16,'tm'=32] {'dp'}, dimensions={0}, use_global_device_ids=true | all-gather | bytes 313344 | tf_op jit(solution)/shard_map/all_gather | solution.py:86
  388.5 0.7 reduce_sum.53
  (52 shorter events, 9.3 us)
Async XLA Ops:
  7.2 114.0 %copy-start = (bf16[3,3,128,128]{3,2,1,0:T(8,128)(2,1)S(1)}, bf16[3,3,128,128]{3,2,1,0:T(8,128)(2,1)}, u32[]{:S(2)}) copy-start(bf16[3,3,128,128]{3,2,1,0:T(8,128)(2,1)} %param.10) | copy-start | bytes 884740
  7.2 13.0 %copy-start.1 = (bf16[1,2,64,16,128]{4,3,2,1,0:T(8,128)(2,1)S(1)}, bf16[1,2,64,16,128]{4,3,2,1,0:T(8,128)(2,1)}, u32[]{:S(2)}) copy-start(bf16[1,2,64,16,128]{4,3,2,1,0:T(8,128)(2,1)} %param.6) | copy-start | bytes 1572868
  7.2 335.1 %all-reduce.6.cloned.1.call-start = ((), (), s32[]{:S(2)}) async-start(), calls=%async_computation.1 | async-start | bytes 1179648
  7.2 13.0 %collective-permute-start = (bf16[1,2,64,16,128]{4,3,2,1,0:T(8,128)(2,1)}, bf16[1,2,64,16,128]{4,3,2,1,0:T(8,128)(2,1)S(1)}, u32[]{:S(2)}, u32[]{:S(2)}) collective-permute-start(bf16[1,2,64,16,128]{4,3,2,1,0:T(8,128)(2,1)} %param.6), channel_id=1, source_target_pairs={{0,1},{1,2},{2,3},{3,4},{4,5},{5,6},{6,7},{7,8},{8,9},{9,10},{10,1... | collective-permute-start | bytes 1572872 | tf_op jit(solution)/shard_map/ppermute | solution.py:12
  30.7 54.5 %copy-start.3 = (f32[128]{0:T(128)S(1)}, f32[128]{0:T(128)}, u32[]{:S(2)}) copy-start(f32[128]{0:T(128)} %param.9) | copy-start | bytes 1540
  30.7 54.5 %copy-start.4 = (f32[128]{0:T(128)S(1)}, f32[128]{0:T(128)}, u32[]{:S(2)}) copy-start(f32[128]{0:T(128)} %param.8) | copy-start | bytes 1540
  106.1 5.8 %collective-permute-start.1 = (bf16[1,64,1,16,128]{4,3,1,2,0:T(8,128)(2,1)S(1)}, bf16[1,64,1,16,128]{4,3,1,2,0:T(8,128)(2,1)S(1)}, u32[]{:S(2)}, u32[]{:S(2)}) collective-permute-start(bf16[1,64,1,16,128]{4,3,1,2,0:T(8,128)(2,1)S(1)} %slice.221), channel_id=1, source_target_pairs={{1,0},{2,1},{3,2},{4,3},{5,4},{6,5},{7,6},{8,7},{9,8},{10,9},{11,1... | collective-permute-start | bytes 786440 | tf_op jit(solution)/shard_map/ppermute | solution.py:12
  117.0 0.9 copy-start.2
Sparse Core Ops, SparseCore 0:
  119.3 222.8 all-reduce.5
